TPU v7x, 32 devices: a whole 2x2x4 slice. The times are simulated.
32 devices in a mesh: ka: 8 (over z, y), col: 4 (over x, core).
Axes of the slice: x: 2, y: 2, z: 4, core: 2. Of those that a mesh axis runs over, the one named last changes fastest.
Arguments:
- amps: bfloat16 [16, 256, 192], P('ka', 'col'), may hold values from -6 to 6
- isdf_coeffs: bfloat16 [16, 2048, 256], P('ka', 'col'), may hold values from -0.375 to 0.375
- w_screen: bfloat16 [16, 2048, 2048], P(None, 'ka', 'col'), as said below
- energies: float32 [16, 256], P('ka', 'col'), may hold values from 0.5 to 3
- qsel: int32 [2], replicated, may hold values from 0 to 15
- partner: int32 [2, 16], replicated, may hold values from 0 to 15, each once within a row
Outputs:
- applied: float32 [16, 256, 192], P('ka', 'col')
Inputs may be any that keep to these rules, and one draw needn't show every extreme that they name: Each row of partner is a permutation of the 16 k points. `w_screen`: each of the 16 matrices is symmetric.
All inputs are finite; a program needn't handle non-finite values.
Results may differ from a plain program's by a relative error of at most 0.013.
Values may be sent and summed in bfloat16 or wider, within the bound.
A program may use at most 64 MiB of HBM per device.

v0:
```python
import jax
import jax.numpy as jnp
from jax import lax
from jax.sharding import PartitionSpec as P


def body(amps, isdf_coeffs, w_screen, energies, qsel, partner):
    k_local = amps.shape[0]
    vectors = amps.shape[2]
    offset_base = lax.axis_index("ka") * k_local
    owned = offset_base + jnp.arange(k_local, dtype=jnp.int32)
    wanted = jnp.take(partner, owned, axis=1).reshape(-1)
    everyone = lax.all_gather(amps, "ka", axis=0, tiled=True)
    picked = jnp.take(everyone, wanted, axis=0)
    partners = lax.all_gather(picked, "col", axis=1, tiled=True)
    partners = partners.reshape(2, k_local, partners.shape[1], vectors)
    densities = jnp.einsum(
        "kms,qkse->qmke", isdf_coeffs, partners, preferred_element_type=jnp.float32
    )
    width = densities.shape[1]
    densities = densities.astype(jnp.bfloat16).reshape(2, width, k_local * vectors)
    slabs = jnp.take(w_screen, qsel, axis=0)
    partials = jnp.einsum(
        "qrm,qmx->qrx",
        lax.all_gather(slabs, "ka", axis=1, tiled=True),
        densities,
        preferred_element_type=jnp.float32,
    )
    screened = lax.psum_scatter(
        partials.astype(jnp.bfloat16), "col", scatter_dimension=1, tiled=True
    ).astype(jnp.float32)
    screened = screened.astype(jnp.bfloat16).reshape(2, width, k_local, vectors)
    projected = jnp.einsum(
        "kms,qmke->kse", isdf_coeffs, screened, preferred_element_type=jnp.float32
    )
    summed = lax.psum_scatter(
        projected.astype(jnp.bfloat16), "col", scatter_dimension=1, tiled=True
    ).astype(jnp.float32)
    return summed + energies[:, :, None] * amps.astype(jnp.float32)


def solution(mesh):
    placed = (
        P("ka", "col", None),
        P("ka", "col", None),
        P(None, "ka", "col"),
        P("ka", "col"),
        P(),
        P(),
    )
    return jax.shard_map(
        body, mesh=mesh, in_specs=placed, out_specs=P("ka", "col", None), check_vma=False
    )
```

profile of v0, /device:TPU:0, one launch (start us, length us, event | category | flops | bytes accessed | tf_op | source)
XLA Modules:
  0.0 176.6 jit_solution(11480643661953069329)
XLA Ops:
  6.5 0.7 compare_select_fusion.4
  7.3 0.7 compare_and_fusion.2
  7.9 2.8 %gather_fusion = bf16[2,256,512]{2,1,0:T(8,128)(2,1)S(1)} fusion(bf16[16,256,512]{2,1,0:T(8,128)(2,1)} %param.8, s32[1024]{0:T(1024)S(1)} %pad_clamp_fusion.2), kind=kCustom, calls=%fused_computation | custom fusion | bytes 1048584 | tf_op jit(solution)/shard_map/jit(_take)/gather | solution.py:22
  10.7 0.9 broadcast_select_fusion
  11.6 0.0 all-gather.2.cloned.1.call-update
  11.7 0.0 reduce-scatter.2.cloned.1.call-start
  11.7 0.8 copy.53
  12.5 0.6 gather_fusion.1
  13.1 0.1 select_bitcast_fusion
  13.1 0.1 copy.54
  13.2 0.1 select_n.71
  13.3 0.1 select_n.69
  13.4 35.6 %all_gather.10 = bf16[16,64,192]{2,1,0:T(8,128)(2,1)S(1)} all-gather(bf16[2,64,192]{2,1,0:T(8,128)(2,1)} %param.6), channel_id=1, replica_groups=mesh['ka'=8,'col'=4] {'ka'}, dimensions={0}, use_global_device_ids=true | all-gather | bytes 442368 | tf_op jit(solution)/shard_map/all_gather | solution.py:13
  49.0 0.6 gather_fusion.2
  49.6 0.1 broadcast_select_fusion.1
  49.7 7.1 %all_gather.11 = bf16[4,256,192]{2,1,0:T(8,128)(2,1)S(1)} all-gather(bf16[4,64,192]{2,1,0:T(8,128)(2,1)S(1)} %broadcast_select_fusion.1), channel_id=1, replica_groups=mesh['ka'=8,'col'=4] {'col'}, dimensions={1}, use_global_device_ids=true | all-gather | bytes 491520 | tf_op jit(solution)/shard_map/all_gather | solution.py:15
  56.8 0.5 fusion
  57.3 0.1 copy.58
  57.4 33.2 %all-gather.2.cloned.1.call-done = bf16[2,2048,512]{2,1,0:T(8,128)(2,1)} async-done(((bf16[2,256,512]{2,1,0:T(8,128)(2,1)}), bf16[2,2048,512]{2,1,0:T(8,128)(2,1)}) %all-gather.2.cloned.1.call-update) | async-done | bytes 4194320 | tf_op jit(solution)/shard_map/all_gather | solution.py:25
  90.6 6.2 %convolution_convert_fusion = bf16[2,2048,384]{2,1,0:T(8,128)(2,1)} fusion(bf16[2,2048,512]{2,1,0:T(8,128)(2,1)} %all-gather.2.cloned.1.call-done, bf16[2,512,384]{1,2,0:T(8,128)(2,1)S(1)} %bitcast.25), kind=kOutput, calls=%fused_computation.3 | convolution fusion | flops 1612185600 | bytes 8126464 | tf_op jit(solution)/shard_map/qrm,qmx->qrx/dot_general | solution.py:23
  96.8 0.0 reduce-scatter.2.cloned.1.call-update
  96.9 0.0 all-reduce.3.cloned.1.call-start
  96.9 36.5 %reduce-scatter.2.cloned.1.call-done = bf16[2,512,384]{2,1,0:T(8,128)(2,1)} async-done(((bf16[2,2048,384]{2,1,0:T(8,128)(2,1)}), bf16[2,512,384]{2,1,0:T(8,128)(2,1)}) %reduce-scatter.2.cloned.1.call-update) | async-done | bytes 786448 | tf_op jit(solution)/shard_map/reduce_scatter | solution.py:29
  133.4 1.2 convert_reduce_fusion
  134.7 0.2 copy.60
  134.9 0.3 fusion.1
  135.1 0.9 copy.61
  136.0 0.0 all-reduce.3.cloned.1.call-update
  136.0 0.6 dynamic-slice
  137.3 31.2 %all-reduce.3.cloned.1.call-done = bf16[2,256,192]{2,0,1:T(2,128)(2,1)} async-done(((bf16[2,256,192]{2,0,1:T(2,128)(2,1)}), bf16[2,256,192]{2,0,1:T(2,128)(2,1)}) %all-reduce.3.cloned.1.call-update) | async-done | bytes 196624
  168.5 0.9 constant_dynamic-slice_fusion
  169.4 0.7 multiply_add_fusion
  (16 shorter events, 0.1 us)
Async XLA Ops:
  6.5 50.3 %copy-start = (bf16[2,512,256]{2,1,0:T(8,128)(2,1)S(1)}, bf16[2,512,256]{2,1,0:T(8,128)(2,1)}, u32[]{:S(2)}) copy-start(bf16[2,512,256]{2,1,0:T(8,128)(2,1)} %param.7) | copy-start | bytes 1572868
  6.5 84.1 %all-gather.2.cloned.1.call-start = ((), (), s32[]{:S(2)}) async-start(), calls=%async_computation.1 | async-start | bytes 4718592 | tf_op jit(solution)/shard_map/all_gather | solution.py:25
  11.7 121.7 %reduce-scatter.2.cloned.1.call-start = ((), (), s32[]{:S(2)}) async-start(), calls=%async_computation.2 | async-start | bytes 3932160 | tf_op jit(solution)/shard_map/reduce_scatter | solution.py:29
  96.8 39.2 %copy-start.3 = (u32[32]{0:T(128)S(1)}, u32[32]{0:T(128)}, u32[]{:S(2)}) copy-start(u32[32]{0:T(128)} %constant.56) | copy-start | bytes 388
  96.8 72.5 %copy-start.1 = (bf16[2,64,192]{2,1,0:T(8,128)(2,1)S(1)}, bf16[2,64,192]{2,1,0:T(8,128)(2,1)}, u32[]{:S(2)}) copy-start(bf16[2,64,192]{2,1,0:T(8,128)(2,1)} %param.6) | copy-start | bytes 147460
  96.8 72.5 %copy-start.2 = (f32[2,64]{1,0:T(2,128)S(1)}, f32[2,64]{1,0:T(2,128)}, u32[]{:S(2)}) copy-start(f32[2,64]{1,0:T(2,128)} %param.9) | copy-start | bytes 1540
  96.9 71.6 %all-reduce.3.cloned.1.call-start = ((), (), s32[]{:S(2)}) async-start(), calls=%async_computation.3 | async-start | bytes 524288
Sparse Core Ops, SparseCore 0:
  11.8 78.7 all-gather.1
  97.0 36.3 reduce-scatter.1
  136.2 32.2 all-reduce.2
where the time goes:
time: 177 us
  waiting for transfers between devices  101 us (57%)
  blocking collectives  42.7 us (24%)
  between operations  13.9 us (8%)
  local copies, waits for them, and re-layouts  7.5 us (4%)
  matrix products  6.98 us (4%)
  other arithmetic  4.51 us (3%)
    reduce_scatter x1, waiting for transfers between devices, body(): lax.psum_scatter(partials.astype(jnp.bfloat16), 'col', scatter_dimension=...  36.5 us
    all_gather x1, blocking collectives, body(): everyone = lax.all_gather(amps, 'ka', axis=0, tiled=True)  35.6 us
    all_gather x1, waiting for transfers between devices, body(): lax.all_gather(slabs, 'ka', axis=1, tiled=True)  33.2 us
    unnamed x4, waiting for transfers between devices  31.2 us
    all_gather x1, blocking collectives, body(): partners = lax.all_gather(picked, 'col', axis=1, tiled=True)  7.1 us
    dot_general x1, matrix products, body(): jnp.einsum('qrm,qmx->qrx', lax.all_gather(slabs, 'ka', axis=1, tiled=True...  6.23 us
  transfers between devices with their start and end apart: 3, of which 3 were waited for; matrix products, arithmetic and copies ran while one was open for 2% of the time, Pallas kernels for 0%

commit v1 on v0

--- a/solution.py
+++ b/solution.py
@@ -10,7 +10,12 @@
     offset_base = lax.axis_index("ka") * k_local
     owned = offset_base + jnp.arange(k_local, dtype=jnp.int32)
     wanted = jnp.take(partner, owned, axis=1).reshape(-1)
-    everyone = lax.all_gather(amps, "ka", axis=0, tiled=True)
+    ring = [amps]
+    for hop in range(7):
+        ring.append(lax.ppermute(ring[-1], "ka", [(dev, (dev + 1) % 8) for dev in range(8)]))
+    everyone = jnp.roll(
+        jnp.concatenate(ring[::-1], axis=0), (lax.axis_index("ka") + 1) * ring[0].shape[0], axis=0
+    )
     picked = jnp.take(everyone, wanted, axis=0)
     partners = lax.all_gather(picked, "col", axis=1, tiled=True)
     partners = partners.reshape(2, k_local, partners.shape[1], vectors)

time: 177 us -> 180 us (1.017)
  blocking collectives: 42.7 us -> 7.51 us
  waiting for transfers between devices: 101 us -> 135 us
  starting transfers between devices: 0.09 us -> 3.15 us
    ppermute x0 -> x7, waiting for transfers between devices: none -> 53.6 us  [body(): lax.ppermute(ring[-1], 'ka', [(dev, (dev + 1) % 8) for dev in range(8)])]
    all_gather x1 -> x0, blocking collectives: 35.6 us -> none  [body(): everyone = lax.all_gather(amps, 'ka', axis=0, tiled=True)]
    all_gather x1, waiting for transfers between devices: 33.2 us -> 13.2 us  [body(): lax.all_gather(slabs, 'ka', axis=1, tiled=True)]
    ppermute x0 -> x7, starting transfers between devices: none -> 3.06 us  [body(): lax.ppermute(ring[-1], 'ka', [(dev, (dev + 1) % 8) for dev in range(8)])]
  transfers between devices with their start and end apart: 3 -> 10, of which waited for: 3 -> 10; matrix products, arithmetic and copies ran while one was open for 2% -> 2% of each run, Pallas kernels for 0% -> 0%
where the time goes in v1:
time: 180 us; the launch traced here: 179 us
  waiting for transfers between devices  135 us (75%)
  between operations  14 us (8%)
  local copies, waits for them, and re-layouts  8.51 us (5%)
  blocking collectives  7.51 us (4%)
  matrix products  6.98 us (4%)
  other arithmetic  4.48 us (2%)
  starting transfers between devices  3.15 us (2%)
    ppermute x7, waiting for transfers between devices, body(): lax.ppermute(ring[-1], 'ka', [(dev, (dev + 1) % 8) for dev in range(8)])  53.6 us
    reduce_scatter x1, waiting for transfers between devices, body(): lax.psum_scatter(partials.astype(jnp.bfloat16), 'col', scatter_dimension=...  36.5 us
    unnamed x4, waiting for transfers between devices  31.3 us
    all_gather x1, waiting for transfers between devices, body(): lax.all_gather(slabs, 'ka', axis=1, tiled=True)  13.2 us
    all_gather x1, blocking collectives, body(): partners = lax.all_gather(picked, 'col', axis=1, tiled=True)  7.51 us
    dot_general x1, matrix products, body(): jnp.einsum('qrm,qmx->qrx', lax.all_gather(slabs, 'ka', axis=1, tiled=True...  6.22 us
  transfers between devices with their start and end apart: 10, of which 10 were waited for; matrix products, arithmetic and copies ran while one was open for 2% of the time, Pallas kernels for 0%

profile of v1, /device:TPU:0, one launch (start us, length us, event | category | flops | bytes accessed | tf_op | source)
XLA Modules:
  0.0 179.2 jit_solution(6853676010807923693)
XLA Ops:
  6.6 0.7 compare_select_fusion.4
  7.3 0.7 compare_and_fusion.2
  8.0 0.8 copy.53
  8.7 0.6 gather_fusion.1
  9.3 0.1 copy.54
  9.4 0.1 select_n.86
  9.5 2.8 %gather_fusion = bf16[2,256,512]{2,1,0:T(8,128)(2,1)S(1)} fusion(bf16[16,256,512]{2,1,0:T(8,128)(2,1)} %param.8, s32[1024]{0:T(1024)S(1)} %get-tuple-element.6), kind=kCustom, calls=%fused_computation | custom fusion | bytes 1048584 | tf_op jit(solution)/shard_map/jit(_take)/gather | solution.py:27
  12.3 0.9 broadcast_select_fusion
  13.3 3.0 %collective-permute-start = (bf16[2,64,192]{2,1,0:T(8,128)(2,1)}, bf16[2,64,192]{2,1,0:T(8,128)(2,1)S(1)}, u32[]{:S(2)}, u32[]{:S(2)}) collective-permute-start(bf16[2,64,192]{2,1,0:T(8,128)(2,1)} %param.6), channel_id=1, source_target_pairs={{0,4},{4,8},{8,12},{12,16},{16,20},{20,24},{24,28},{28,0},{1,5},{5... | collective-permute-start | bytes 147464 | tf_op jit(solution)/shard_map/ppermute | solution.py:15
  16.3 5.5 %collective-permute-done = bf16[2,64,192]{2,1,0:T(8,128)(2,1)S(1)} collective-permute-done((bf16[2,64,192]{2,1,0:T(8,128)(2,1)}, bf16[2,64,192]{2,1,0:T(8,128)(2,1)S(1)}, u32[]{:S(2)}, u32[]{:S(2)}) %collective-permute-start) | collective-permute-done | bytes 49184 | tf_op jit(solution)/shard_map/ppermute | solution.py:15
  21.8 7.1 %collective-permute-done.1 = bf16[2,64,192]{2,1,0:T(8,128)(2,1)S(1)} collective-permute-done((bf16[2,64,192]{2,1,0:T(8,128)(2,1)S(1)}, bf16[2,64,192]{2,1,0:T(8,128)(2,1)S(1)}, u32[]{:S(2)}, u32[]{:S(2)}) %collective-permute-start.1) | collective-permute-done | bytes 49184 | tf_op jit(solution)/shard_map/ppermute | solution.py:15
  28.9 8.5 %collective-permute-done.2 = bf16[2,64,192]{2,1,0:T(8,128)(2,1)S(1)} collective-permute-done((bf16[2,64,192]{2,1,0:T(8,128)(2,1)S(1)}, bf16[2,64,192]{2,1,0:T(8,128)(2,1)S(1)}, u32[]{:S(2)}, u32[]{:S(2)}) %collective-permute-start.2) | collective-permute-done | bytes 49184 | tf_op jit(solution)/shard_map/ppermute | solution.py:15
  37.4 8.5 %collective-permute-done.3 = bf16[2,64,192]{2,1,0:T(8,128)(2,1)S(1)} collective-permute-done((bf16[2,64,192]{2,1,0:T(8,128)(2,1)S(1)}, bf16[2,64,192]{2,1,0:T(8,128)(2,1)S(1)}, u32[]{:S(2)}, u32[]{:S(2)}) %collective-permute-start.3) | collective-permute-done | bytes 49184 | tf_op jit(solution)/shard_map/ppermute | solution.py:15
  45.9 7.0 %collective-permute-done.4 = bf16[2,64,192]{2,1,0:T(8,128)(2,1)S(1)} collective-permute-done((bf16[2,64,192]{2,1,0:T(8,128)(2,1)S(1)}, bf16[2,64,192]{2,1,0:T(8,128)(2,1)S(1)}, u32[]{:S(2)}, u32[]{:S(2)}) %collective-permute-start.4) | collective-permute-done | bytes 49184 | tf_op jit(solution)/shard_map/ppermute | solution.py:15
  53.0 8.6 %collective-permute-done.5 = bf16[2,64,192]{2,1,0:T(8,128)(2,1)S(1)} collective-permute-done((bf16[2,64,192]{2,1,0:T(8,128)(2,1)S(1)}, bf16[2,64,192]{2,1,0:T(8,128)(2,1)S(1)}, u32[]{:S(2)}, u32[]{:S(2)}) %collective-permute-start.5) | collective-permute-done | bytes 49184 | tf_op jit(solution)/shard_map/ppermute | solution.py:15
  61.6 8.5 %collective-permute-done.6 = bf16[2,64,192]{2,1,0:T(8,128)(2,1)S(1)} collective-permute-done((bf16[2,64,192]{2,1,0:T(8,128)(2,1)S(1)}, bf16[2,64,192]{2,1,0:T(8,128)(2,1)S(1)}, u32[]{:S(2)}, u32[]{:S(2)}) %collective-permute-start.6) | collective-permute-done | bytes 49184 | tf_op jit(solution)/shard_map/ppermute | solution.py:15
  70.2 0.8 constant_dynamic-update-slice_fusion.8
  71.2 0.6 gather_fusion.2
  71.8 0.1 broadcast_select_fusion.1
  71.8 7.5 %all_gather.7 = bf16[4,256,192]{2,1,0:T(8,128)(2,1)S(1)} all-gather(bf16[4,64,192]{2,1,0:T(8,128)(2,1)S(1)} %broadcast_select_fusion.1), channel_id=1, replica_groups=mesh['ka'=8,'col'=4] {'col'}, dimensions={1}, use_global_device_ids=true | all-gather | bytes 491520 | tf_op jit(solution)/shard_map/all_gather | solution.py:20
  79.4 0.5 fusion
  79.9 13.2 %all-gather.2.cloned.1.call-done = bf16[2,2048,512]{2,1,0:T(8,128)(2,1)} async-done(((bf16[2,256,512]{2,1,0:T(8,128)(2,1)}), bf16[2,2048,512]{2,1,0:T(8,128)(2,1)}) %all-gather.2.cloned.1.call-update) | async-done | bytes 4194320 | tf_op jit(solution)/shard_map/all_gather | solution.py:30
  93.1 6.2 %convolution_convert_fusion = bf16[2,2048,384]{2,1,0:T(8,128)(2,1)} fusion(bf16[2,2048,512]{2,1,0:T(8,128)(2,1)} %all-gather.2.cloned.1.call-done, bf16[2,512,384]{1,2,0:T(8,128)(2,1)S(1)} %bitcast.25), kind=kOutput, calls=%fused_computation.3 | convolution fusion | flops 1612185600 | bytes 8126464 | tf_op jit(solution)/shard_map/qrm,qmx->qrx/dot_general | solution.py:28
  99.4 36.5 %reduce-scatter.2.cloned.1.call-done = bf16[2,512,384]{2,1,0:T(8,128)(2,1)} async-done(((bf16[2,2048,384]{2,1,0:T(8,128)(2,1)}), bf16[2,512,384]{2,1,0:T(8,128)(2,1)}) %reduce-scatter.2.cloned.1.call-update) | async-done | bytes 786448 | tf_op jit(solution)/shard_map/reduce_scatter | solution.py:34
  135.9 1.2 convert_reduce_fusion
  137.2 0.2 copy.60
  137.4 0.3 fusion.1
  137.7 0.9 copy.61
  138.6 0.6 dynamic-slice
  139.8 31.2 %all-reduce.3.cloned.1.call-done = bf16[2,256,192]{2,0,1:T(2,128)(2,1)} async-done(((bf16[2,256,192]{2,0,1:T(2,128)(2,1)}), bf16[2,256,192]{2,0,1:T(2,128)(2,1)}) %all-reduce.3.cloned.1.call-update) | async-done | bytes 196624
  171.0 0.9 constant_dynamic-slice_fusion
  171.9 0.7 multiply_add_fusion
  (45 shorter events, 0.6 us)
Async XLA Ops:
  6.5 72.8 %copy-start = (bf16[2,512,256]{2,1,0:T(8,128)(2,1)S(1)}, bf16[2,512,256]{2,1,0:T(8,128)(2,1)}, u32[]{:S(2)}) copy-start(bf16[2,512,256]{2,1,0:T(8,128)(2,1)} %param.7) | copy-start | bytes 1572868
  6.5 64.6 %copy-start.1 = (bf16[2,64,192]{2,1,0:T(8,128)(2,1)S(1)}, bf16[2,64,192]{2,1,0:T(8,128)(2,1)}, u32[]{:S(2)}) copy-start(bf16[2,64,192]{2,1,0:T(8,128)(2,1)} %param.6) | copy-start | bytes 147460
  6.5 86.6 %all-gather.2.cloned.1.call-start = ((), (), s32[]{:S(2)}) async-start(), calls=%async_computation.1 | async-start | bytes 4718592 | tf_op jit(solution)/shard_map/all_gather | solution.py:30
  13.3 122.7 %reduce-scatter.2.cloned.1.call-start = ((), (), s32[]{:S(2)}) async-start(), calls=%async_computation.2 | async-start | bytes 3932160 | tf_op jit(solution)/shard_map/reduce_scatter | solution.py:34
  13.3 8.5 %collective-permute-start = (bf16[2,64,192]{2,1,0:T(8,128)(2,1)}, bf16[2,64,192]{2,1,0:T(8,128)(2,1)S(1)}, u32[]{:S(2)}, u32[]{:S(2)}) collective-permute-start(bf16[2,64,192]{2,1,0:T(8,128)(2,1)} %param.6), channel_id=1, source_target_pairs={{0,4},{4,8},{8,12},{12,16},{16,20},{20,24},{24,28},{28,0},{1,5},{5... | collective-permute-start | bytes 147464 | tf_op jit(solution)/shard_map/ppermute | solution.py:15
  21.8 7.1 %collective-permute-start.1 = (bf16[2,64,192]{2,1,0:T(8,128)(2,1)S(1)}, bf16[2,64,192]{2,1,0:T(8,128)(2,1)S(1)}, u32[]{:S(2)}, u32[]{:S(2)}) collective-permute-start(bf16[2,64,192]{2,1,0:T(8,128)(2,1)S(1)} %collective-permute-done), channel_id=1, source_target_pairs={{0,4},{4,8},{8,12},{12,16},{16,20},{20,24},{24,28},{28,0},{1,5},{5... | collective-permute-start | bytes 147464 | tf_op jit(solution)/shard_map/ppermute | solution.py:15
  28.9 8.5 %collective-permute-start.2 = (bf16[2,64,192]{2,1,0:T(8,128)(2,1)S(1)}, bf16[2,64,192]{2,1,0:T(8,128)(2,1)S(1)}, u32[]{:S(2)}, u32[]{:S(2)}) collective-permute-start(bf16[2,64,192]{2,1,0:T(8,128)(2,1)S(1)} %collective-permute-done.1), channel_id=1, source_target_pairs={{0,4},{4,8},{8,12},{12,16},{16,20},{20,24},{24,28},{28,0},{1,5},{5... | collective-permute-start | bytes 147464 | tf_op jit(solution)/shard_map/ppermute | solution.py:15
  37.4 8.5 %collective-permute-start.3 = (bf16[2,64,192]{2,1,0:T(8,128)(2,1)S(1)}, bf16[2,64,192]{2,1,0:T(8,128)(2,1)S(1)}, u32[]{:S(2)}, u32[]{:S(2)}) collective-permute-start(bf16[2,64,192]{2,1,0:T(8,128)(2,1)S(1)} %collective-permute-done.2), channel_id=1, source_target_pairs={{0,4},{4,8},{8,12},{12,16},{16,20},{20,24},{24,28},{28,0},{1,5},{5... | collective-permute-start | bytes 147464 | tf_op jit(solution)/shard_map/ppermute | solution.py:15
  45.9 7.0 %collective-permute-start.4 = (bf16[2,64,192]{2,1,0:T(8,128)(2,1)S(1)}, bf16[2,64,192]{2,1,0:T(8,128)(2,1)S(1)}, u32[]{:S(2)}, u32[]{:S(2)}) collective-permute-start(bf16[2,64,192]{2,1,0:T(8,128)(2,1)S(1)} %collective-permute-done.3), channel_id=1, source_target_pairs={{0,4},{4,8},{8,12},{12,16},{16,20},{20,24},{24,28},{28,0},{1,5},{5... | collective-permute-start | bytes 147464 | tf_op jit(solution)/shard_map/ppermute | solution.py:15
  52.9 8.7 %collective-permute-start.5 = (bf16[2,64,192]{2,1,0:T(8,128)(2,1)S(1)}, bf16[2,64,192]{2,1,0:T(8,128)(2,1)S(1)}, u32[]{:S(2)}, u32[]{:S(2)}) collective-permute-start(bf16[2,64,192]{2,1,0:T(8,128)(2,1)S(1)} %collective-permute-done.4), channel_id=1, source_target_pairs={{0,4},{4,8},{8,12},{12,16},{16,20},{20,24},{24,28},{28,0},{1,5},{5... | collective-permute-start | bytes 147464 | tf_op jit(solution)/shard_map/ppermute | solution.py:15
  61.6 8.5 %collective-permute-start.6 = (bf16[2,64,192]{2,1,0:T(8,128)(2,1)S(1)}, bf16[2,64,192]{2,1,0:T(8,128)(2,1)S(1)}, u32[]{:S(2)}, u32[]{:S(2)}) collective-permute-start(bf16[2,64,192]{2,1,0:T(8,128)(2,1)S(1)} %collective-permute-done.5), channel_id=1, source_target_pairs={{0,4},{4,8},{8,12},{12,16},{16,20},{20,24},{24,28},{28,0},{1,5},{5... | collective-permute-start | bytes 147464 | tf_op jit(solution)/shard_map/ppermute | solution.py:15
  99.3 39.2 %copy-start.3 = (u32[32]{0:T(128)S(1)}, u32[32]{0:T(128)}, u32[]{:S(2)}) copy-start(u32[32]{0:T(128)} %constant.77) | copy-start | bytes 388
  99.3 72.6 %copy-start.2 = (f32[2,64]{1,0:T(2,128)S(1)}, f32[2,64]{1,0:T(2,128)}, u32[]{:S(2)}) copy-start(f32[2,64]{1,0:T(2,128)} %param.9) | copy-start | bytes 1540
  99.4 71.6 %all-reduce.3.cloned.1.call-start = ((), (), s32[]{:S(2)}) async-start(), calls=%async_computation.3 | async-start | bytes 524288
Sparse Core Ops, SparseCore 0:
  13.4 79.6 all-gather.1
  99.5 36.3 reduce-scatter.1
  138.7 32.2 all-reduce.2
